TPU v7x, 32 devices: a whole 2x2x4 slice. The times are simulated.
32 devices in a mesh: rows: 8 (over z, core), pairs: 4 (over y, x).
Axes of the slice: x: 2, y: 2, z: 4, core: 2. Of those that a mesh axis runs over, the one named last changes fastest.
Arguments:
- observed: float32 [12288, 2048], P('rows', 'pairs'), as said below
- estimate: float32 [12288, 2048], P('rows', 'pairs'), may hold values from -0.054126587 to 0.054126587
- mask: int32 [12288, 2048], P('rows', 'pairs'), may hold values from 0 to 1
- threshold: float32 [2048], P('pairs'), may hold values from 0.02 to 0.12
Outputs:
- regrouped: float32 [2048, 12288], P(('rows', 'pairs'))
Inputs may be any that keep to these rules, and one draw needn't show every extreme that they name: observed has entries of order 12288^-1/2.
All inputs are finite; a program needn't handle non-finite values.
Results may differ from a plain program's by a relative error of at most 0.0003.
Values sent between devices are 32-bit elements; how exact they have to be, the bound alone decides.
A program may use at most 128 MiB of HBM per device.

v0:
```python
import functools

import jax
import jax.numpy as jnp
from jax import lax
from jax.experimental import pallas as pl
from jax.experimental.pallas import tpu as pltpu
from jax.sharding import PartitionSpec as P

MESH = pl.DeviceIdType.MESH
F32 = jnp.float32
BF16 = jnp.bfloat16
NN = (((1,), (0,)), ((), ()))
NT = (((1,), (1,)), ((), ()))


def split(a):
    high = a.astype(BF16)
    return high, (a - high.astype(F32)).astype(BF16)


def dot_parts(a, b, dims):
    def one(x, y):
        return lax.dot_general(x, y, dims, preferred_element_type=F32)

    return one(a[0], b[0]) + (one(a[0], b[1]) + one(a[1], b[0]))


def dot3(a, b, dims=NN):
    return dot_parts(split(a), split(b), dims)


def whitening_t(gram):
    width = gram.shape[0]
    eye = (
        lax.broadcasted_iota(jnp.int32, (width, width), 0)
        == lax.broadcasted_iota(jnp.int32, (width, width), 1)
    ).astype(F32)
    on_diag = gram * eye
    d_col = jnp.sum(on_diag, axis=1, keepdims=True) + 1e-06
    d_row = jnp.sum(on_diag, axis=0, keepdims=True) + 1e-06
    i_col = 1.0 / jnp.sqrt(d_col)
    i_row = 1.0 / jnp.sqrt(d_row)
    normed = gram * i_col * i_row
    sq = jnp.sum(jnp.sum(normed * normed, axis=1, keepdims=True), axis=0, keepdims=True)
    fro = jnp.sqrt(sq)
    y = normed / fro
    t = 1.5 * eye - 0.5 * y
    z = t
    y = dot3(y, t)
    t = 1.5 * eye - 0.5 * dot3(z, y)
    y, z = dot3(y, t), dot3(t, z)
    t = 1.5 * eye - 0.5 * dot3(z, y)
    z = dot3(t, z)
    return jnp.sqrt(d_col) * z * i_row / jnp.sqrt(fro)


def join(ss, sm, mm):
    top = jnp.concatenate([ss, sm], axis=1)
    low = jnp.concatenate([sm.T, mm], axis=1)
    return jnp.concatenate([top, low], axis=0)


def kernel(
    n_rows, n_pairs, step,
    obs_ref, est_ref, mask_ref, thr_ref, out_ref,
    obs_in, est_in, mask_in, x, perm, pay, land, res, gmm_out, gmm_in, send,
    rs_s, rs_r, ag_s, ag_r, pm_s, pm_r, pg_s, pg_r, out_s, out_r, own_sem, in_sem,
):
    me = lax.axis_index("rows")
    group = lax.axis_index("pairs")
    n = n_rows * n_pairs
    bw = x.shape[2]
    rows = x.shape[3]
    chunks = rows // step
    each = send.shape[1]

    def fetches(half):
        cols = pl.ds(half * 2 * bw, 2 * bw)
        pairs = ((obs_ref, obs_in), (est_ref, est_in), (mask_ref, mask_in))
        return [
            pltpu.make_async_copy(src.at[:, cols], dst.at[:, cols], in_sem.at[half, i])
            for i, (src, dst) in enumerate(pairs)
        ]

    for half in (1, 0):
        for fetch in fetches(half):
            fetch.start()

    barrier = pltpu.get_barrier_semaphore()
    my_k = me * n_pairs + group

    def greet(i, carry):
        k = lax.rem(my_k + i, n)
        pl.semaphore_signal(
            barrier, inc=1, device_id=(k // n_pairs, lax.rem(k, n_pairs)), device_id_type=MESH
        )
        return carry

    lax.fori_loop(1, n, greet, 0)

    def fill(half):
        for fetch in fetches(half):
            fetch.wait()
        for slot in (2 * half, 2 * half + 1):
            cols = slice(slot * bw, (slot + 1) * bw)
            for c in range(chunks):
                part = slice(c * step, (c + 1) * step)
                filled = jnp.where(mask_in[part, cols] == 1, obs_in[part, cols], est_in[part, cols])
                x[0, slot, :, part] = filled.T

    def full_gram(s, m):
        total = jnp.zeros((2 * bw, 2 * bw), F32)
        for c in range(chunks):
            part = slice(c * step, (c + 1) * step)
            both = split(jnp.concatenate([s[:, part], m[:, part]], axis=0))
            total += dot_parts(both, both, NT)
        return total

    def cross_gram(s, m):
        total = jnp.zeros((bw, bw), F32)
        for c in range(chunks):
            part = slice(c * step, (c + 1) * step)
            total += dot_parts(split(s[:, part]), split(m[:, part]), NT)
        return total

    def place(b):
        base = sum(COUNTS[:b]) * bw
        piece = COUNTS[b] * bw // n_rows
        return base, base // n_rows, piece

    def own(b, p):
        base, _, piece = place(b)
        return pl.ds(pl.multiple_of(base + p * piece, 8), piece)

    def others(b):
        _, lbase, piece = place(b)
        return land.at[pl.ds(1, n_rows - 1), pl.ds(lbase, piece)]

    def reduce_start(b, blocks):
        base, lbase, piece = place(b)
        for i, block in enumerate(blocks):
            pay[base + i * bw : base + (i + 1) * bw, :] = block
        if b == 0:
            pl.semaphore_wait(barrier, n - 1)

        def scatter(off, carry):
            peer = lax.rem(me + off, n_rows)
            pltpu.make_async_remote_copy(
                pay.at[own(b, peer)], land.at[off, pl.ds(lbase, piece)],
                rs_s.at[b], rs_r.at[b], device_id=(peer, group), device_id_type=MESH,
            ).start()
            return carry

        lax.fori_loop(1, n_rows, scatter, 0)

    def reduce_mid(b):
        _, lbase, piece = place(b)
        pltpu.make_async_copy(others(b), others(b), rs_r.at[b]).wait()
        mine = own(b, me)
        total = pay[mine, :]
        for off in range(1, n_rows):
            total += land[off, lbase : lbase + piece, :]
        res[mine, :] = total

        def gather(off, carry):
            peer = lax.rem(me + off, n_rows)
            pltpu.make_async_remote_copy(
                res.at[mine], res.at[mine],
                ag_s.at[b], ag_r.at[b], device_id=(peer, group), device_id_type=MESH,
            ).start()
            return carry

        lax.fori_loop(1, n_rows, gather, 0)

    def reduce_end(b):
        base, _, _ = place(b)
        pltpu.make_async_copy(others(b), others(b), ag_r.at[b]).wait()
        return [res[base + i * bw : base + (i + 1) * bw, :] for i in range(COUNTS[b])]

    def settle(b):
        pltpu.make_async_copy(others(b), others(b), rs_s.at[b]).wait()
        pltpu.make_async_copy(others(b), others(b), ag_s.at[b]).wait()

    def put(v_half, s, m, write):
        v_parts = split(v_half)
        for c in range(chunks):
            part = slice(c * step, (c + 1) * step)
            both = split(jnp.concatenate([s[:, part], m[:, part]], axis=0))
            write(part, dot_parts(v_parts, both, NN))

    def into(ref):
        def write(part, value):
            ref[:, part] = value
        return write

    right = lax.rem(group + 1, n_pairs)

    def pass_copy(src, dst, send_sem, recv_sem):
        return pltpu.make_async_remote_copy(
            src, dst, send_sem, recv_sem, device_id=(me, right), device_id_type=MESH
        )

    def put_and_pass(i, v_half, s, m, block):
        def write(part, value):
            block[:, part] = value
            pass_copy(block.at[:, part], perm.at[i, :, part], pm_s.at[i], pm_r.at[i]).start()

        put(v_half, s, m, write)

    def pass_gram(i, block, gmm):
        gmm_out[i] = gmm
        small = pass_copy(gmm_out.at[i], gmm_in.at[i], pg_s.at[i], pg_r.at[i])
        small.start()
        return pass_copy(block, perm.at[i], pm_s.at[i], pm_r.at[i]), small

    def new_grams(v, gram):
        vg = dot3(v, gram)
        return dot3(vg[:bw], v[:bw], NT), dot3(vg[bw:], v[bw:], NT)

    def deliver(half):
        count = n // 2

        def go(i, carry):
            k = half * count + lax.rem(my_k + i, count)

            @pl.when(k != my_k)
            def _():
                pltpu.make_async_remote_copy(
                    send.at[k], out_ref.at[my_k], out_s, out_r,
                    device_id=(k // n_pairs, lax.rem(k, n_pairs)), device_id_type=MESH,
                ).start()

            @pl.when(k == my_k)
            def _():
                pltpu.make_async_copy(send.at[k], out_ref.at[my_k], own_sem).start()

            return carry

        lax.fori_loop(0, count, go, 0)

    def finish(half, v, gram, s, m):
        vg = dot3(v, gram)
        squares = jnp.sum(vg * v, axis=1, keepdims=True)
        norm = jnp.sqrt(squares + 1e-06)
        eye = (
            lax.broadcasted_iota(jnp.int32, gram.shape, 0)
            == lax.broadcasted_iota(jnp.int32, gram.shape, 1)
        )
        level = thr_ref[:, 2 * half * bw : 2 * (half + 1) * bw]
        level = jnp.sum(jnp.where(eye, level, 0.0), axis=1, keepdims=True)
        scaled = (jnp.maximum(norm - level, 0.0) / norm) * v
        per_block = bw // each
        for j in range(2):
            def write(part, value):
                for i in range(per_block):
                    send[(2 * half + j) * per_block + i, :, part] = value[i * each : (i + 1) * each]
            put(scaled[j * bw : (j + 1) * bw], s, m, write)

    def thirds(g):
        return [g[:bw, :bw], g[:bw, bw:], g[bw:, bw:]]

    fill(1)
    reduce_start(0, thirds(full_gram(x.at[0, 2], x.at[0, 3])))
    fill(0)
    reduce_start(1, thirds(full_gram(x.at[0, 0], x.at[0, 1])))
    reduce_mid(0)
    reduce_mid(1)
    gb = join(*reduce_end(0))
    vb = whitening_t(gb)
    put_and_pass(0, vb[bw:], x.at[0, 2], x.at[0, 3], x.at[1, 3])
    bs, bm = new_grams(vb, gb)
    sent = [pass_gram(0, x.at[1, 3], bm)]
    put(vb[:bw], x.at[0, 2], x.at[0, 3], into(x.at[1, 2]))
    ga = join(*reduce_end(1))
    va = whitening_t(ga)
    put(va[bw:], x.at[0, 0], x.at[0, 1], into(x.at[1, 1]))

    reduce_start(2, [cross_gram(x.at[1, 2], x.at[1, 1])])
    put(va[:bw], x.at[0, 0], x.at[0, 1], into(x.at[1, 0]))
    reduce_mid(2)
    as_, am = new_grams(va, ga)
    gb = join(bs, *reduce_end(2), am)
    vb = whitening_t(gb)
    put_and_pass(1, vb[bw:], x.at[1, 2], x.at[1, 1], x.at[2, 3])
    bs, bm = new_grams(vb, gb)
    sent.append(pass_gram(1, x.at[2, 3], bm))

    for c in sent[0]:
        c.wait_recv()
    reduce_start(3, [cross_gram(x.at[1, 0], perm.at[0])])
    put(vb[:bw], x.at[1, 2], x.at[1, 1], into(x.at[2, 2]))
    reduce_mid(3)
    ga = join(as_, *reduce_end(3), gmm_in[0])
    va = whitening_t(ga)
    put(va[bw:], x.at[1, 0], perm.at[0], into(x.at[2, 1]))

    reduce_start(4, [cross_gram(x.at[2, 2], x.at[2, 1])])
    put(va[:bw], x.at[1, 0], perm.at[0], into(x.at[2, 0]))
    as_, am = new_grams(va, ga)
    for c in sent[1]:
        c.wait_recv()
    reduce_mid(4)
    reduce_start(5, [cross_gram(x.at[2, 0], perm.at[1])])
    gb = join(bs, *reduce_end(4), am)
    reduce_mid(5)
    vb = whitening_t(gb)
    put_and_pass(2, vb[bw:], x.at[2, 2], x.at[2, 1], x.at[3, 3])
    bs, bm = new_grams(vb, gb)
    sent.append(pass_gram(2, x.at[3, 3], bm))
    put(vb[:bw], x.at[2, 2], x.at[2, 1], into(x.at[3, 2]))
    ga = join(as_, *reduce_end(5), gmm_in[1])
    va = whitening_t(ga)
    put(va[bw:], x.at[2, 0], perm.at[1], into(x.at[3, 1]))

    reduce_start(6, [cross_gram(x.at[3, 2], x.at[3, 1])])
    put(va[:bw], x.at[2, 0], perm.at[1], into(x.at[3, 0]))
    as_, am = new_grams(va, ga)
    reduce_mid(6)
    gb = join(bs, *reduce_end(6), am)
    vb = whitening_t(gb)
    for c in sent[2]:
        c.wait_recv()
    reduce_start(7, [cross_gram(x.at[3, 0], perm.at[2])])
    finish(1, vb, gb, x.at[3, 2], x.at[3, 1])
    reduce_mid(7)
    ga = join(as_, *reduce_end(7), gmm_in[2])
    deliver(1)
    finish(0, whitening_t(ga), ga, x.at[3, 0], perm.at[2])
    deliver(0)

    for b in range(len(COUNTS)):
        settle(b)
    for pair in sent:
        for c in pair:
            c.wait_send()
    pltpu.make_async_copy(send.at[0], out_ref.at[my_k], own_sem).wait()
    rest = send.at[pl.ds(0, n - 1)]
    pltpu.make_async_copy(rest, rest, out_s).wait()
    arrived = out_ref.at[pl.ds(0, n - 1)]
    pltpu.make_async_copy(arrived, arrived, out_r).wait()


def interleave(in_ref, out_ref):
    n_pairs, each, _ = in_ref.shape
    for i in range(each):
        out_ref[i * n_pairs : (i + 1) * n_pairs, :] = in_ref[:, i, :]


COUNTS = (3, 3, 1, 1, 1, 1, 1, 1)


def on_device(observed, estimate, mask, threshold):
    n_rows = lax.axis_size("rows")
    n_pairs = lax.axis_size("pairs")
    rows, width = observed.shape
    bw = width // 4
    n = n_rows * n_pairs
    each = width // n
    step = 512 if rows % 512 == 0 else rows
    total = sum(COUNTS) * bw
    vmem = pl.BlockSpec(memory_space=pltpu.VMEM)
    dma = pltpu.SemaphoreType.DMA
    nb = len(COUNTS)
    landed = pl.pallas_call(
        functools.partial(kernel, n_rows, n_pairs, step),
        out_shape=jax.ShapeDtypeStruct((n, each, rows), F32),
        in_specs=[pl.BlockSpec(memory_space=pl.ANY)] * 3 + [vmem],
        out_specs=pl.BlockSpec(memory_space=pl.ANY),
        scratch_shapes=[
            pltpu.VMEM((rows, width), F32),
            pltpu.VMEM((rows, width), F32),
            pltpu.VMEM((rows, width), jnp.int32),
            pltpu.VMEM((4, 4, bw, rows), F32),
            pltpu.VMEM((3, bw, rows), F32),
            pltpu.VMEM((total, bw), F32),
            pltpu.VMEM((n_rows, total // n_rows, bw), F32),
            pltpu.VMEM((total, bw), F32),
            pltpu.VMEM((3, bw, bw), F32),
            pltpu.VMEM((3, bw, bw), F32),
            pltpu.VMEM((n, each, rows), F32),
            dma((nb,)), dma((nb,)), dma((nb,)), dma((nb,)),
            dma((3,)), dma((3,)), dma((3,)), dma((3,)),
            dma, dma, dma, dma((2, 3)),
        ],
        compiler_params=pltpu.CompilerParams(
            collective_id=0, has_side_effects=True, vmem_limit_bytes=60 * 1024 * 1024
        ),
    )(observed, estimate, mask, threshold.reshape(1, width))
    landed = landed.reshape(n_rows, n_pairs, each, rows)
    return pl.pallas_call(
        interleave,
        grid=(n_rows,),
        out_shape=jax.ShapeDtypeStruct((each * n_pairs, n_rows * rows), F32),
        in_specs=[pl.BlockSpec((None, n_pairs, each, rows), lambda r: (r, 0, 0, 0))],
        out_specs=pl.BlockSpec((each * n_pairs, rows), lambda r: (0, r)),
    )(landed)


def solution(mesh):
    placed = (P("rows", "pairs"), P("rows", "pairs"), P("rows", "pairs"), P("pairs"))
    return jax.shard_map(
        on_device, mesh=mesh, in_specs=placed, out_specs=P(("rows", "pairs"), None), check_vma=False
    )
```

profile of v0, /device:TPU:0, one launch (start us, length us, event | category | flops | bytes accessed | tf_op | source)
XLA Modules:
  0.0 181.4 jit_solution(16181936911477815859)
XLA Ops:
  0.0 175.0 %shard_map.46 = f32[32,16,1536]{2,1,0:T(8,128)} custom-call(f32[1536,512]{1,0:T(8,128)} %obs_ref.1, f32[1536,512]{1,0:T(8,128)} %est_ref.1, s32[1536,512]{1,0:T(8,128)} %mask_ref.1, f32[1,512]{1,0:T(1,128)} %bitcast.3), custom_call_target="tpu_custom_call" | custom-call | tf_op jit(solution)/shard_map/pallas_call | solution.py:365
  175.0 6.4 %shard_map.47 = f32[64,12288]{1,0:T(8,128)} custom-call(f32[8,4,16,1536]{3,2,1,0:T(8,128)} %bitcast.2), custom_call_target="tpu_custom_call" | custom-call | tf_op jit(solution)/shard_map/pallas_call | solution.py:391
where the time goes:
time: 182 us; the launch traced here: 181 us
  Pallas kernels  181 us (99%)
    pallas_call x1, Pallas kernels, on_device(): pl.pallas_call(functools.partial(kernel, n_rows, n_pairs, step), out_shap...  175 us
    pallas_call x1, Pallas kernels, on_device(): pl.pallas_call(interleave, grid=(n_rows,), out_shape=jax.ShapeDtypeStruct...  6.41 us

commit v1 on v0

v1 whole, which is shorter than its diff:
```python
import functools

import jax
import jax.numpy as jnp
from jax import lax
from jax.experimental import pallas as pl
from jax.experimental.pallas import tpu as pltpu
from jax.sharding import PartitionSpec as P

MESH = pl.DeviceIdType.MESH
F32 = jnp.float32
BF16 = jnp.bfloat16
NN = (((1,), (0,)), ((), ()))
NT = (((1,), (1,)), ((), ()))


def split(a):
    high = a.astype(BF16)
    return high, (a - high.astype(F32)).astype(BF16)


def dot_parts(a, b, dims):
    def one(x, y):
        return lax.dot_general(x, y, dims, preferred_element_type=F32)

    return one(a[0], b[0]) + (one(a[0], b[1]) + one(a[1], b[0]))


def dot3(a, b, dims=NN):
    return dot_parts(split(a), split(b), dims)


def whitening_t(gram):
    width = gram.shape[0]
    eye = (
        lax.broadcasted_iota(jnp.int32, (width, width), 0)
        == lax.broadcasted_iota(jnp.int32, (width, width), 1)
    ).astype(F32)
    on_diag = gram * eye
    d_col = jnp.sum(on_diag, axis=1, keepdims=True) + 1e-06
    d_row = jnp.sum(on_diag, axis=0, keepdims=True) + 1e-06
    i_col = 1.0 / jnp.sqrt(d_col)
    i_row = 1.0 / jnp.sqrt(d_row)
    normed = gram * i_col * i_row
    sq = jnp.sum(jnp.sum(normed * normed, axis=1, keepdims=True), axis=0, keepdims=True)
    fro = jnp.sqrt(sq)
    y = normed / fro
    t = 1.5 * eye - 0.5 * y
    z = t
    y = dot3(y, t)
    t = 1.5 * eye - 0.5 * dot3(z, y)
    y, z = dot3(y, t), dot3(t, z)
    t = 1.5 * eye - 0.5 * dot3(z, y)
    z = dot3(t, z)
    return jnp.sqrt(d_col) * z * i_row / jnp.sqrt(fro)


def join(ss, sm, mm):
    top = jnp.concatenate([ss, sm], axis=1)
    low = jnp.concatenate([sm.T, mm], axis=1)
    return jnp.concatenate([top, low], axis=0)


def square(width):
    shape = (width, width)
    return lax.broadcasted_iota(jnp.int32, shape, 0), lax.broadcasted_iota(jnp.int32, shape, 1)


def pack(gram, n_own):
    bw = gram.shape[0] // 2
    ss, sm, mm = gram[:bw, :bw], gram[:bw, bw:], gram[bw:, bw:]
    r, c = square(bw)
    diag = jnp.sum(jnp.where(r == c, mm, 0.0), axis=0, keepdims=True)
    return [jnp.where(r <= c, ss, mm), sm, jnp.broadcast_to(diag, (8 * n_own, bw))]


def unpack(packed):
    bw = packed.shape[1]
    both, sm, diag = packed[:bw], packed[bw : 2 * bw], packed[2 * bw : 2 * bw + 1]
    r, c = square(bw)
    flip = both.T
    mm = jnp.where(r == c, diag, jnp.where(r > c, both, flip))
    return join(jnp.where(r <= c, both, flip), sm, mm)


def owners(n_rows):
    return (n_rows // 4, n_rows // 2) if n_rows % 4 == 0 else (0, n_rows)


def sizes_of(bw, n_own):
    return [2 * bw + 8 * n_own] * 2 + [bw] * 6


def kernel(
    n_rows, n_pairs, step, early,
    obs_ref, est_ref, mask_ref, thr_ref, out_ref,
    obs_in, est_in, mask_in, x, keep, pay, land, res, gmm_out, gmm_in, last_hi, last_lo, send, far, onward,
    rs_s, rs_r, ag_s, ag_r, pm_s, pm_r, pg_s, pg_r, out_s, out_r, own_sem, in_sem, far_s, far_r,
):
    me = lax.axis_index("rows")
    group = lax.axis_index("pairs")
    n = n_rows * n_pairs
    bw = x.shape[2]
    rows = x.shape[3]
    chunks = rows // step
    each = send.shape[1]
    count = n // 2
    side = me // (n_rows // 2)
    partner = lax.rem(me + n_rows // 2, n_rows)
    partner_k = partner * n_pairs + group
    first, n_own = owners(n_rows)
    owner = (me >= first) & (me < first + n_own)
    sizes = sizes_of(bw, n_own)

    def fetches(half):
        cols = pl.ds(half * 2 * bw, 2 * bw)
        pairs = ((obs_ref, obs_in), (est_ref, est_in), (mask_ref, mask_in))
        return [
            pltpu.make_async_copy(src.at[:, cols], dst.at[:, cols], in_sem.at[half, i])
            for i, (src, dst) in enumerate(pairs)
        ]

    for half in (1, 0):
        for fetch in fetches(half):
            fetch.start()

    barrier = pltpu.get_barrier_semaphore()
    my_k = me * n_pairs + group

    def greet(i, carry):
        k = lax.rem(my_k + i, n)
        pl.semaphore_signal(
            barrier, inc=1, device_id=(k // n_pairs, lax.rem(k, n_pairs)), device_id_type=MESH
        )
        return carry

    lax.fori_loop(1, n, greet, 0)

    def fill(half):
        for fetch in fetches(half):
            fetch.wait()
        for slot in (2 * half, 2 * half + 1):
            cols = slice(slot * bw, (slot + 1) * bw)
            for c in range(chunks):
                part = slice(c * step, (c + 1) * step)
                filled = jnp.where(mask_in[part, cols] == 1, obs_in[part, cols], est_in[part, cols])
                x[0, slot, :, part] = filled.T

    def full_gram(s, m):
        total = jnp.zeros((2 * bw, 2 * bw), F32)
        for c in range(chunks):
            part = slice(c * step, (c + 1) * step)
            both = split(jnp.concatenate([s[:, part], m[:, part]], axis=0))
            total += dot_parts(both, both, NT)
        return total

    def cross_gram(s, m):
        total = jnp.zeros((2 * bw, 2 * bw), F32)
        for c in range(chunks):
            part = slice(c * step, (c + 1) * step)
            s_parts = jnp.concatenate(split(s[:, part]), axis=0)
            m_parts = jnp.concatenate(split(m[:, part]), axis=0)
            total += lax.dot_general(s_parts, m_parts, NT, preferred_element_type=F32)
        return total[:bw, :bw] + (total[:bw, bw:] + total[bw:, :bw])

    def place(b):
        return sum(sizes[:b]), sum(sizes[:b]) // n_own, sizes[b] // n_own

    def own(b, q):
        base, _, piece = place(b)
        return pl.ds(pl.multiple_of(base + q * piece, 8), piece)

    def fill_pay(b, blocks):
        at = place(b)[0]
        for block in blocks:
            pay[at : at + block.shape[0], :] = block
            at += block.shape[0]

    def reduce_start(b, blocks=()):
        _, lbase, piece = place(b)
        fill_pay(b, blocks)
        if b == 0:
            pl.semaphore_wait(barrier, n - 1)

        def scatter(i, carry):
            q = lax.rem(me + i, n_own)
            peer = first + q

            @pl.when(peer != me)
            def _():
                pltpu.make_async_remote_copy(
                    pay.at[own(b, q)], land.at[lax.rem(me + n_rows - peer, n_rows), pl.ds(lbase, piece)],
                    rs_s.at[b], rs_r.at[b], device_id=(peer, group), device_id_type=MESH,
                ).start()

            return carry

        lax.fori_loop(0, n_own, scatter, 0)

    def wait_pieces(b, some, sem):
        _, lbase, piece = place(b)
        ref = land.at[pl.ds(0, some), pl.ds(lbase, piece)]
        pltpu.make_async_copy(ref, ref, sem).wait()

    def reduce_mid(b):
        _, lbase, piece = place(b)

        @pl.when(owner)
        def _():
            wait_pieces(b, n_rows - 1, rs_r.at[b])
            mine = own(b, me - first)
            total = pay[mine, :]
            for off in range(1, n_rows):
                total += land[off, lbase : lbase + piece, :]
            res[mine, :] = total

            def gather(off, carry):
                peer = lax.rem(me + off, n_rows)
                pltpu.make_async_remote_copy(
                    res.at[mine], res.at[mine],
                    ag_s.at[b], ag_r.at[b], device_id=(peer, group), device_id_type=MESH,
                ).start()
                return carry

            lax.fori_loop(1, n_rows, gather, 0)

    def pieces_to_owners(b, sem):
        @pl.when(owner)
        def _():
            wait_pieces(b, n_own - 1, sem)

        @pl.when(jnp.logical_not(owner))
        def _():
            wait_pieces(b, n_own, sem)

    def reduce_end(b):
        base, _, _ = place(b)
        pieces_to_owners(b, ag_r.at[b])
        return res[base : base + sizes[b], :]

    def settle(b):
        pieces_to_owners(b, rs_s.at[b])

        @pl.when(owner)
        def _():
            wait_pieces(b, n_rows - 1, ag_s.at[b])

    def put(v_parts, s, m, write, start=0, stop=None):
        stop = s.shape[1] if stop is None else stop
        for at in range(start, stop, step):
            part = slice(at, min(at + step, stop))
            both = split(jnp.concatenate([s[:, part], m[:, part]], axis=0))
            write(part, dot_parts(v_parts, both, NN))

    def into(ref):
        def write(part, value):
            ref[:, part] = value
        return write

    right = lax.rem(group + 1, n_pairs)

    def pass_copy(src, dst, send_sem, recv_sem):
        return pltpu.make_async_remote_copy(
            src, dst, send_sem, recv_sem, device_id=(me, right), device_id_type=MESH
        )

    def put_and_pass(i, v_half, s, m):
        def write(part, value):
            keep[i, :, part] = value
            pass_copy(
                keep.at[i, :, part], x.at[i + 1, 1, :, part], pm_s.at[i], pm_r.at[i]
            ).start()

        put(split(v_half), s, m, write)

    def pass_gram(i, gmm):
        gmm_out[i] = gmm
        small = pass_copy(gmm_out.at[i], gmm_in.at[i], pg_s.at[i], pg_r.at[i])
        small.start()
        return pass_copy(keep.at[i], x.at[i + 1, 1], pm_s.at[i], pm_r.at[i]), small

    def new_grams(v, gram):
        vg = dot3(v, gram)
        return dot3(vg[:bw], v[:bw], NT), dot3(vg[bw:], v[bw:], NT)

    n_early = early // 128

    def far_copy(half, j, at, size):
        return pltpu.make_async_remote_copy(
            x.at[3, 2 * half + j, :, pl.ds(at, size)], far.at[j, :, pl.ds(at, size)],
            far_s.at[j], far_r.at[j], device_id=(partner, group), device_id_type=MESH,
        )

    shipped = [0, 0]

    def ship(half, some):
        for i in range(shipped[half], min(shipped[half] + some, 2 * n_early)):
            @pl.when(side != half)
            def _():
                far_copy(half, i // n_early, i % n_early * 128, 128).start()
        shipped[half] += some

    def scale_last(half, v, gram):
        vg = dot3(v, gram)
        squares = jnp.sum(vg * v, axis=1, keepdims=True)
        norm = jnp.sqrt(squares + 1e-06)
        eye = (
            lax.broadcasted_iota(jnp.int32, gram.shape, 0)
            == lax.broadcasted_iota(jnp.int32, gram.shape, 1)
        )
        level = thr_ref[:, 2 * half * bw : 2 * (half + 1) * bw]
        level = jnp.sum(jnp.where(eye, level, 0.0), axis=1, keepdims=True)
        last_hi[half], last_lo[half] = split((jnp.maximum(norm - level, 0.0) / norm) * v)

    per_block = bw // each

    def finish(half, target, base, s, m, start, stop):
        for j in range(2):
            def write(part, value):
                for i in range(per_block):
                    target[base + j * per_block + i, :, part] = value[i * each : (i + 1) * each]

            cut = slice(j * bw, (j + 1) * bw)
            put((last_hi[half, cut], last_lo[half, cut]), s, m, write, start, stop)

    def to(k):
        return dict(device_id=(k // n_pairs, lax.rem(k, n_pairs)), device_id_type=MESH)

    def deliver(half, same):
        def go(i, carry):
            k = half * count + lax.rem(my_k + i, count)
            if not same:
                pltpu.make_async_remote_copy(
                    send.at[k, :, early:], out_ref.at[my_k, :, early:], out_s.at[1], out_r.at[1], **to(k)
                ).start()
                return carry

            @pl.when(k != my_k)
            def _():
                pltpu.make_async_remote_copy(
                    send.at[k], out_ref.at[my_k], out_s.at[0], out_r.at[0], **to(k)
                ).start()

            @pl.when(k == my_k)
            def _():
                pltpu.make_async_copy(send.at[k], out_ref.at[my_k], own_sem.at[0]).start()

            return carry

        lax.fori_loop(0, count, go, 0)

    def deliver_onward():
        def go(i, carry):
            at = lax.rem(my_k + i, count)
            k = side * count + at
            spot = out_ref.at[partner_k, :, :early]

            @pl.when(k != my_k)
            def _():
                pltpu.make_async_remote_copy(
                    onward.at[at], spot, out_s.at[2], out_r.at[2], **to(k)
                ).start()

            @pl.when(k == my_k)
            def _():
                pltpu.make_async_copy(onward.at[at], spot, own_sem.at[1]).start()

            return carry

        lax.fori_loop(0, count, go, 0)

    fill(1)
    reduce_start(0, pack(full_gram(x.at[0, 2], x.at[0, 3]), n_own))
    fill(0)
    fill_pay(1, pack(full_gram(x.at[0, 0], x.at[0, 1]), n_own))
    reduce_mid(0)
    reduce_start(1)
    gb = unpack(reduce_end(0))
    vb = whitening_t(gb)
    put_and_pass(0, vb[bw:], x.at[0, 2], x.at[0, 3])
    reduce_mid(1)
    bs, bm = new_grams(vb, gb)
    sent = [pass_gram(0, bm)]
    put(split(vb[:bw]), x.at[0, 2], x.at[0, 3], into(x.at[1, 2]))
    ga = unpack(reduce_end(1))
    va = whitening_t(ga)
    put(split(va[bw:]), x.at[0, 0], x.at[0, 1], into(x.at[1, 3]))

    reduce_start(2, [cross_gram(x.at[1, 2], x.at[1, 3])])
    put(split(va[:bw]), x.at[0, 0], x.at[0, 1], into(x.at[1, 0]))
    as_, am = new_grams(va, ga)
    reduce_mid(2)
    gb = join(bs, reduce_end(2), am)
    vb = whitening_t(gb)
    put_and_pass(1, vb[bw:], x.at[1, 2], x.at[1, 3])
    for c in sent[0]:
        c.wait_recv()
    reduce_start(3, [cross_gram(x.at[1, 0], x.at[1, 1])])
    bs, bm = new_grams(vb, gb)
    sent.append(pass_gram(1, bm))
    put(split(vb[:bw]), x.at[1, 2], x.at[1, 3], into(x.at[2, 2]))
    reduce_mid(3)
    ga = join(as_, reduce_end(3), gmm_in[0])
    va = whitening_t(ga)
    put(split(va[bw:]), x.at[1, 0], x.at[1, 1], into(x.at[2, 3]))

    reduce_start(4, [cross_gram(x.at[2, 2], x.at[2, 3])])
    put(split(va[:bw]), x.at[1, 0], x.at[1, 1], into(x.at[2, 0]))
    as_, am = new_grams(va, ga)
    reduce_mid(4)
    gb = join(bs, reduce_end(4), am)
    for c in sent[1]:
        c.wait_recv()
    reduce_start(5, [cross_gram(x.at[2, 0], x.at[2, 1])])
    vb = whitening_t(gb)
    put_and_pass(2, vb[bw:], x.at[2, 2], x.at[2, 3])
    bs, bm = new_grams(vb, gb)
    sent.append(pass_gram(2, bm))
    put(split(vb[:bw]), x.at[2, 2], x.at[2, 3], into(x.at[3, 2]))
    ship(1, SHIP[0])
    reduce_mid(5)
    ship(1, SHIP[1])
    ga = join(as_, reduce_end(5), gmm_in[1])
    va = whitening_t(ga)
    put(split(va[bw:]), x.at[2, 0], x.at[2, 1], into(x.at[3, 3]))

    reduce_start(6, [cross_gram(x.at[3, 2], x.at[3, 3])])
    ship(1, SHIP[2])
    put(split(va[:bw]), x.at[2, 0], x.at[2, 1], into(x.at[3, 0]))
    ship(0, SHIP[3])
    as_, am = new_grams(va, ga)
    reduce_mid(6)
    ship(1, SHIP[4])
    ship(0, min(SHIP[5], n_early - SHIP[3]))
    for c in sent[2]:
        c.wait_recv()
    reduce_start(7, [cross_gram(x.at[3, 0], x.at[3, 1])])
    ship(1, SHIP[6])
    ship(0, SHIP[7])
    gb = join(bs, reduce_end(6), am)
    scale_last(1, whitening_t(gb), gb)
    reduce_mid(7)
    ship(1, 2 * n_early)
    ship(0, 2 * n_early)
    ga = join(as_, reduce_end(7), gmm_in[2])
    scale_last(0, whitening_t(ga), ga)

    for half in (1, 0):
        @pl.when(side != half)
        def _():
            finish(half, send, half * count, x.at[3, 2 * half], x.at[3, 2 * half + 1], early, rows)
            deliver(half, False)

    for half in (1, 0):
        @pl.when(side == half)
        def _():
            finish(half, send, half * count, x.at[3, 2 * half], x.at[3, 2 * half + 1], 0, rows)
            deliver(half, True)
            for j in range(2):
                far_copy(half, j, 0, early).wait_recv()
            finish(half, onward, 0, far.at[0], far.at[1], 0, early)
            deliver_onward()

    for b in range(len(sizes)):
        settle(b)
    for pair in sent:
        for c in pair:
            c.wait_send()
    for j in range(2):
        far_copy(0, j, 0, early).wait_send()
    pltpu.make_async_copy(send.at[0], out_ref.at[my_k], own_sem.at[0]).wait()
    pltpu.make_async_copy(onward.at[0], out_ref.at[my_k, :, :early], own_sem.at[1]).wait()
    for ref, sems in ((send, out_s), (out_ref, out_r)):
        for i, some in enumerate((
            ref.at[pl.ds(0, count - 1)],
            ref.at[pl.ds(0, count), :, early:],
            ref.at[pl.ds(0, count - 1), :, :early],
        )):
            pltpu.make_async_copy(some, some, sems.at[i]).wait()


def interleave(in_ref, out_ref):
    n_pairs, each, _ = in_ref.shape
    for i in range(each):
        out_ref[i * n_pairs : (i + 1) * n_pairs, :] = in_ref[:, i, :]


SHIP = (1, 1, 2, 1, 1, 3, 2, 1)


def on_device(observed, estimate, mask, threshold):
    n_rows = lax.axis_size("rows")
    n_pairs = lax.axis_size("pairs")
    rows, width = observed.shape
    bw = width // 4
    n = n_rows * n_pairs
    each = width // n
    step = 512 if rows % 512 == 0 else rows
    early = rows * 5 // 12 // 128 * 128 or rows
    n_own = owners(n_rows)[1]
    sizes = sizes_of(bw, n_own)
    total = sum(sizes)
    vmem = pl.BlockSpec(memory_space=pltpu.VMEM)
    dma = pltpu.SemaphoreType.DMA
    nb = len(sizes)
    landed = pl.pallas_call(
        functools.partial(kernel, n_rows, n_pairs, step, early),
        out_shape=jax.ShapeDtypeStruct((n, each, rows), F32),
        in_specs=[pl.BlockSpec(memory_space=pl.ANY)] * 3 + [vmem],
        out_specs=pl.BlockSpec(memory_space=pl.ANY),
        scratch_shapes=[
            pltpu.VMEM((rows, width), F32),
            pltpu.VMEM((rows, width), F32),
            pltpu.VMEM((rows, width), jnp.int32),
            pltpu.VMEM((4, 4, bw, rows), F32),
            pltpu.VMEM((3, bw, rows), F32),
            pltpu.VMEM((total, bw), F32),
            pltpu.VMEM((n_rows, total // n_own, bw), F32),
            pltpu.VMEM((total, bw), F32),
            pltpu.VMEM((3, bw, bw), F32),
            pltpu.VMEM((3, bw, bw), F32),
            pltpu.VMEM((2, 2 * bw, 2 * bw), BF16),
            pltpu.VMEM((2, 2 * bw, 2 * bw), BF16),
            pltpu.VMEM((n, each, rows), F32),
            pltpu.VMEM((2, bw, early), F32),
            pltpu.VMEM((n // 2, each, early), F32),
            dma((nb,)), dma((nb,)), dma((nb,)), dma((nb,)),
            dma((3,)), dma((3,)), dma((3,)), dma((3,)),
            dma((3,)), dma((3,)), dma((2,)), dma((2, 3)), dma((2,)), dma((2,)),
        ],
        compiler_params=pltpu.CompilerParams(
            collective_id=0, has_side_effects=True, vmem_limit_bytes=60 * 1024 * 1024
        ),
    )(observed, estimate, mask, threshold.reshape(1, width))
    landed = landed.reshape(n_rows, n_pairs, each, rows)
    return pl.pallas_call(
        interleave,
        grid=(n_rows,),
        out_shape=jax.ShapeDtypeStruct((each * n_pairs, n_rows * rows), F32),
        in_specs=[pl.BlockSpec((None, n_pairs, each, rows), lambda r: (r, 0, 0, 0))],
        out_specs=pl.BlockSpec((each * n_pairs, rows), lambda r: (0, r)),
    )(landed)


def solution(mesh):
    placed = (P("rows", "pairs"), P("rows", "pairs"), P("rows", "pairs"), P("pairs"))
    return jax.shard_map(
        on_device, mesh=mesh, in_specs=placed, out_specs=P(("rows", "pairs"), None), check_vma=False
    )
```

time: 182 us -> 161 us (0.88); the launches traced: 181 us -> 158 us
  Pallas kernels: 181 us -> 158 us
    pallas_call x1, Pallas kernels: 175 us -> 152 us  [on_device(): pl.pallas_call(functools.partial(kernel, n_rows, n_pairs, step, early), o...]
where the time goes in v1:
time: 161 us; the launch traced here: 158 us
  Pallas kernels  158 us (98%)
    pallas_call x1, Pallas kernels, on_device(): pl.pallas_call(functools.partial(kernel, n_rows, n_pairs, step, early), o...  152 us
    pallas_call x1, Pallas kernels, on_device(): pl.pallas_call(interleave, grid=(n_rows,), out_shape=jax.ShapeDtypeStruct...  6.41 us

profile of v1, /device:TPU:0, one launch (start us, length us, event | category | flops | bytes accessed | tf_op | source)
XLA Modules:
  0.0 158.1 jit_solution(15629470981805910742)
XLA Ops:
  0.0 151.6 %shard_map.46 = f32[32,16,1536]{2,1,0:T(8,128)} custom-call(f32[1536,512]{1,0:T(8,128)} %obs_ref.1, f32[1536,512]{1,0:T(8,128)} %est_ref.1, s32[1536,512]{1,0:T(8,128)} %mask_ref.1, f32[1,512]{1,0:T(1,128)} %bitcast.3), custom_call_target="tpu_custom_call" | custom-call | tf_op jit(solution)/shard_map/pallas_call | solution.py:506
  151.6 6.4 %shard_map.47 = f32[64,12288]{1,0:T(8,128)} custom-call(f32[8,4,16,1536]{3,2,1,0:T(8,128)} %bitcast.2), custom_call_target="tpu_custom_call" | custom-call | tf_op jit(solution)/shard_map/pallas_call | solution.py:536

commit v2 on v1

--- a/solution.py
+++ b/solution.py
@@ -92,10 +92,11 @@
 
 
 def kernel(
-    n_rows, n_pairs, step, early,
+    n_rows, n_pairs, step, early, ahead,
     obs_ref, est_ref, mask_ref, thr_ref, out_ref,
-    obs_in, est_in, mask_in, x, keep, pay, land, res, gmm_out, gmm_in, last_hi, last_lo, send, far, onward,
+    obs_in, est_in, mask_in, x, keep, pay, land, res, gmm_out, gmm_in, last_hi, last_lo, send, far, onward, raw, v_out, v_in,
     rs_s, rs_r, ag_s, ag_r, pm_s, pm_r, pg_s, pg_r, out_s, out_r, own_sem, in_sem, far_s, far_r,
+    raw_s, raw_r, v_s, v_r,
 ):
     me = lax.axis_index("rows")
     group = lax.axis_index("pairs")
@@ -112,17 +113,21 @@
     owner = (me >= first) & (me < first + n_own)
     sizes = sizes_of(bw, n_own)
 
-    def fetches(half):
+    def fetches(half, c):
         cols = pl.ds(half * 2 * bw, 2 * bw)
+        part = pl.ds(c * step, step)
         pairs = ((obs_ref, obs_in), (est_ref, est_in), (mask_ref, mask_in))
         return [
-            pltpu.make_async_copy(src.at[:, cols], dst.at[:, cols], in_sem.at[half, i])
+            pltpu.make_async_copy(src.at[part, cols], dst.at[part, cols], in_sem.at[half, c, i])
             for i, (src, dst) in enumerate(pairs)
         ]
 
-    for half in (1, 0):
-        for fetch in fetches(half):
-            fetch.start()
+    def fetch_start(half):
+        for c in range(chunks):
+            for fetch in fetches(half, c):
+                fetch.start()
+
+    fetch_start(1)
 
     barrier = pltpu.get_barrier_semaphore()
     my_k = me * n_pairs + group
@@ -136,21 +141,19 @@
 
     lax.fori_loop(1, n, greet, 0)
 
-    def fill(half):
-        for fetch in fetches(half):
-            fetch.wait()
-        for slot in (2 * half, 2 * half + 1):
-            cols = slice(slot * bw, (slot + 1) * bw)
-            for c in range(chunks):
-                part = slice(c * step, (c + 1) * step)
-                filled = jnp.where(mask_in[part, cols] == 1, obs_in[part, cols], est_in[part, cols])
-                x[0, slot, :, part] = filled.T
-
-    def full_gram(s, m):
+    fetch_start(0)
+
+    def fill_gram(half):
         total = jnp.zeros((2 * bw, 2 * bw), F32)
         for c in range(chunks):
             part = slice(c * step, (c + 1) * step)
-            both = split(jnp.concatenate([s[:, part], m[:, part]], axis=0))
+            for fetch in fetches(half, c):
+                fetch.wait()
+            for slot in (2 * half, 2 * half + 1):
+                cols = slice(slot * bw, (slot + 1) * bw)
+                filled = jnp.where(mask_in[part, cols] == 1, obs_in[part, cols], est_in[part, cols])
+                x[0, slot, :, part] = filled.T
+            both = split(jnp.concatenate([x[0, 2 * half, :, part], x[0, 2 * half + 1, :, part]], axis=0))
             total += dot_parts(both, both, NT)
         return total
 
@@ -264,6 +267,8 @@
             src, dst, send_sem, recv_sem, device_id=(me, right), device_id_type=MESH
         )
 
+    skip = (ahead, 0, 0)
+
     def put_and_pass(i, v_half, s, m):
         def write(part, value):
             keep[i, :, part] = value
@@ -271,13 +276,31 @@
                 keep.at[i, :, part], x.at[i + 1, 1, :, part], pm_s.at[i], pm_r.at[i]
             ).start()
 
-        put(split(v_half), s, m, write)
+        put(split(v_half), s, m, write, skip[i])
 
     def pass_gram(i, gmm):
         gmm_out[i] = gmm
         small = pass_copy(gmm_out.at[i], gmm_in.at[i], pg_s.at[i], pg_r.at[i])
         small.start()
-        return pass_copy(keep.at[i], x.at[i + 1, 1], pm_s.at[i], pm_r.at[i]), small
+        main = pass_copy(
+            keep.at[i, :, skip[i] :], x.at[i + 1, 1, :, skip[i] :], pm_s.at[i], pm_r.at[i]
+        )
+        return main, small
+
+    raw_copy = pass_copy(x.at[0, 2:4, :, :ahead], raw, raw_s, raw_r)
+    odd = lax.rem(me, 2)
+    sibling = me + 1 - 2 * odd
+    mine_v = pl.ds(pl.multiple_of(odd * (bw // 2), 8), bw // 2)
+    other_v = pl.ds(pl.multiple_of((1 - odd) * (bw // 2), 8), bw // 2)
+    v_pass = pass_copy(v_out.at[mine_v], v_in.at[mine_v], v_s.at[0], v_r.at[0])
+    v_share = pltpu.make_async_remote_copy(
+        v_in.at[mine_v], v_in.at[mine_v], v_s.at[1], v_r.at[1],
+        device_id=(sibling, group), device_id_type=MESH,
+    )
+    v_shared = pltpu.make_async_remote_copy(
+        v_in.at[other_v], v_in.at[other_v], v_s.at[1], v_r.at[1],
+        device_id=(sibling, group), device_id_type=MESH,
+    )
 
     def new_grams(v, gram):
         vg = dot3(v, gram)
@@ -369,16 +392,34 @@
 
         lax.fori_loop(0, count, go, 0)
 
-    fill(1)
-    reduce_start(0, pack(full_gram(x.at[0, 2], x.at[0, 3]), n_own))
-    fill(0)
-    fill_pay(1, pack(full_gram(x.at[0, 0], x.at[0, 1]), n_own))
+    def compute_last(half):
+        s, m = x.at[3, 2 * half], x.at[3, 2 * half + 1]
+        finish(half, send, half * count, s, m, early, rows)
+
+        @pl.when(side == half)
+        def _():
+            finish(half, send, half * count, s, m, 0, early)
+
+    def deliver_last(half):
+        @pl.when(side != half)
+        def _():
+            deliver(half, False)
+
+        @pl.when(side == half)
+        def _():
+            deliver(half, True)
+
+    reduce_start(0, pack(fill_gram(1), n_own))
+    raw_copy.start()
+    fill_pay(1, pack(fill_gram(0), n_own))
+    reduce_start(1)
     reduce_mid(0)
-    reduce_start(1)
+    reduce_mid(1)
     gb = unpack(reduce_end(0))
     vb = whitening_t(gb)
+    v_out[...] = vb[bw:]
+    v_pass.start()
     put_and_pass(0, vb[bw:], x.at[0, 2], x.at[0, 3])
-    reduce_mid(1)
     bs, bm = new_grams(vb, gb)
     sent = [pass_gram(0, bm)]
     put(split(vb[:bw]), x.at[0, 2], x.at[0, 3], into(x.at[1, 2]))
@@ -388,11 +429,16 @@
 
     reduce_start(2, [cross_gram(x.at[1, 2], x.at[1, 3])])
     put(split(va[:bw]), x.at[0, 0], x.at[0, 1], into(x.at[1, 0]))
+    v_pass.wait_recv()
+    v_share.start()
     as_, am = new_grams(va, ga)
     reduce_mid(2)
     gb = join(bs, reduce_end(2), am)
     vb = whitening_t(gb)
     put_and_pass(1, vb[bw:], x.at[1, 2], x.at[1, 3])
+    raw_copy.wait_recv()
+    v_shared.wait_recv()
+    put(split(v_in[...]), raw.at[0], raw.at[1], into(x.at[1, 1]))
     for c in sent[0]:
         c.wait_recv()
     reduce_start(3, [cross_gram(x.at[1, 0], x.at[1, 1])])
@@ -408,10 +454,10 @@
     put(split(va[:bw]), x.at[1, 0], x.at[1, 1], into(x.at[2, 0]))
     as_, am = new_grams(va, ga)
     reduce_mid(4)
-    gb = join(bs, reduce_end(4), am)
     for c in sent[1]:
         c.wait_recv()
     reduce_start(5, [cross_gram(x.at[2, 0], x.at[2, 1])])
+    gb = join(bs, reduce_end(4), am)
     vb = whitening_t(gb)
     put_and_pass(2, vb[bw:], x.at[2, 2], x.at[2, 3])
     bs, bm = new_grams(vb, gb)
@@ -439,23 +485,18 @@
     ship(0, SHIP[7])
     gb = join(bs, reduce_end(6), am)
     scale_last(1, whitening_t(gb), gb)
+    compute_last(1)
     reduce_mid(7)
     ship(1, 2 * n_early)
     ship(0, 2 * n_early)
     ga = join(as_, reduce_end(7), gmm_in[2])
+    deliver_last(1)
     scale_last(0, whitening_t(ga), ga)
-
-    for half in (1, 0):
-        @pl.when(side != half)
-        def _():
-            finish(half, send, half * count, x.at[3, 2 * half], x.at[3, 2 * half + 1], early, rows)
-            deliver(half, False)
-
+    compute_last(0)
+    deliver_last(0)
     for half in (1, 0):
         @pl.when(side == half)
         def _():
-            finish(half, send, half * count, x.at[3, 2 * half], x.at[3, 2 * half + 1], 0, rows)
-            deliver(half, True)
             for j in range(2):
                 far_copy(half, j, 0, early).wait_recv()
             finish(half, onward, 0, far.at[0], far.at[1], 0, early)
@@ -466,6 +507,9 @@
     for pair in sent:
         for c in pair:
             c.wait_send()
+    raw_copy.wait_send()
+    v_pass.wait_send()
+    v_share.wait_send()
     for j in range(2):
         far_copy(0, j, 0, early).wait_send()
     pltpu.make_async_copy(send.at[0], out_ref.at[my_k], own_sem.at[0]).wait()
@@ -479,10 +523,21 @@
             pltpu.make_async_copy(some, some, sems.at[i]).wait()
 
 
-def interleave(in_ref, out_ref):
-    n_pairs, each, _ = in_ref.shape
-    for i in range(each):
-        out_ref[i * n_pairs : (i + 1) * n_pairs, :] = in_ref[:, i, :]
+def interleave(in_ref, out_ref, taken, mixed, in_sem, out_sem):
+    n_rows, n_pairs, each, rows = in_ref.shape
+    ins = [pltpu.make_async_copy(in_ref.at[r], taken.at[r], in_sem.at[r]) for r in range(n_rows)]
+    for copy in ins:
+        copy.start()
+    outs = []
+    for r in range(n_rows):
+        cols = slice(r * rows, (r + 1) * rows)
+        ins[r].wait()
+        for i in range(each):
+            mixed[i * n_pairs : (i + 1) * n_pairs, cols] = taken[r, :, i, :]
+        outs.append(pltpu.make_async_copy(mixed.at[:, cols], out_ref.at[:, cols], out_sem.at[r]))
+        outs[-1].start()
+    for copy in outs:
+        copy.wait()
 
 
 SHIP = (1, 1, 2, 1, 1, 3, 2, 1)
@@ -496,7 +551,8 @@
     n = n_rows * n_pairs
     each = width // n
     step = 512 if rows % 512 == 0 else rows
-    early = rows * 5 // 12 // 128 * 128 or rows
+    early = rows * 4 // 12 // 128 * 128 or rows
+    ahead = rows * 5 // 12 // 128 * 128 or rows
     n_own = owners(n_rows)[1]
     sizes = sizes_of(bw, n_own)
     total = sum(sizes)
@@ -504,7 +560,7 @@
     dma = pltpu.SemaphoreType.DMA
     nb = len(sizes)
     landed = pl.pallas_call(
-        functools.partial(kernel, n_rows, n_pairs, step, early),
+        functools.partial(kernel, n_rows, n_pairs, step, early, ahead),
         out_shape=jax.ShapeDtypeStruct((n, each, rows), F32),
         in_specs=[pl.BlockSpec(memory_space=pl.ANY)] * 3 + [vmem],
         out_specs=pl.BlockSpec(memory_space=pl.ANY),
@@ -524,9 +580,13 @@
             pltpu.VMEM((n, each, rows), F32),
             pltpu.VMEM((2, bw, early), F32),
             pltpu.VMEM((n // 2, each, early), F32),
+            pltpu.VMEM((2, bw, ahead), F32),
+            pltpu.VMEM((bw, 2 * bw), F32),
+            pltpu.VMEM((bw, 2 * bw), F32),
             dma((nb,)), dma((nb,)), dma((nb,)), dma((nb,)),
             dma((3,)), dma((3,)), dma((3,)), dma((3,)),
-            dma((3,)), dma((3,)), dma((2,)), dma((2, 3)), dma((2,)), dma((2,)),
+            dma((3,)), dma((3,)), dma((2,)), dma((2, rows // step, 3)), dma((2,)), dma((2,)),
+            dma, dma, dma((2,)), dma((2,)),
         ],
         compiler_params=pltpu.CompilerParams(
             collective_id=0, has_side_effects=True, vmem_limit_bytes=60 * 1024 * 1024
@@ -535,10 +595,14 @@
     landed = landed.reshape(n_rows, n_pairs, each, rows)
     return pl.pallas_call(
         interleave,
-        grid=(n_rows,),
         out_shape=jax.ShapeDtypeStruct((each * n_pairs, n_rows * rows), F32),
-        in_specs=[pl.BlockSpec((None, n_pairs, each, rows), lambda r: (r, 0, 0, 0))],
-        out_specs=pl.BlockSpec((each * n_pairs, rows), lambda r: (0, r)),
+        in_specs=[pl.BlockSpec(memory_space=pl.ANY)],
+        out_specs=pl.BlockSpec(memory_space=pl.ANY),
+        scratch_shapes=[
+            pltpu.VMEM((n_rows, n_pairs, each, rows), F32),
+            pltpu.VMEM((each * n_pairs, n_rows * rows), F32),
+            dma((n_rows,)), dma((n_rows,)),
+        ],
     )(landed)
 
 

time: 161 us -> 150 us (0.932); the launches traced: 158 us -> 150 us
  Pallas kernels: 158 us -> 150 us
    pallas_call x2, Pallas kernels: 158 us -> 150 us  [the longest x1 147 us: on_device(): pl.pallas_call(functools.partial(kernel, n_rows, n_pairs, step, early, ah...]
where the time goes in v2:
time: 150 us
  Pallas kernels  150 us (100%)
    pallas_call x1, Pallas kernels, on_device(): pl.pallas_call(functools.partial(kernel, n_rows, n_pairs, step, early, ah...  147 us

profile of v2, /device:TPU:0, one launch (start us, length us, event | category | flops | bytes accessed | tf_op | source)
XLA Modules:
  0.0 150.2 jit_solution(14727426435239633478)
XLA Ops:
  0.0 147.1 %shard_map.46 = f32[32,16,1536]{2,1,0:T(8,128)} custom-call(f32[1536,512]{1,0:T(8,128)} %obs_ref.1, f32[1536,512]{1,0:T(8,128)} %est_ref.1, s32[1536,512]{1,0:T(8,128)} %mask_ref.1, f32[1,512]{1,0:T(1,128)} %bitcast.3), custom_call_target="tpu_custom_call" | custom-call | tf_op jit(solution)/shard_map/pallas_call | solution.py:562
  147.1 2.9 %shard_map.47 = f32[64,12288]{1,0:T(8,128)} custom-call(f32[8,4,16,1536]{3,2,1,0:T(8,128)} %bitcast.2), custom_call_target="tpu_custom_call" | custom-call | tf_op jit(solution)/shard_map/pallas_call | solution.py:596

commit v3 on v2

--- a/solution.py
+++ b/solution.py
@@ -42,16 +42,16 @@
     i_col = 1.0 / jnp.sqrt(d_col)
     i_row = 1.0 / jnp.sqrt(d_row)
     normed = gram * i_col * i_row
-    sq = jnp.sum(jnp.sum(normed * normed, axis=1, keepdims=True), axis=0, keepdims=True)
+    sq = jnp.sum(jnp.sum(normed * normed, axis=0, keepdims=True), axis=1, keepdims=True)
     fro = jnp.sqrt(sq)
     y = normed / fro
+    square_y = dot3(y, y)
     t = 1.5 * eye - 0.5 * y
-    z = t
-    y = dot3(y, t)
-    t = 1.5 * eye - 0.5 * dot3(z, y)
-    y, z = dot3(y, t), dot3(t, z)
-    t = 1.5 * eye - 0.5 * dot3(z, y)
-    z = dot3(t, z)
+    square_t = 2.25 * eye - 1.5 * y + 0.25 * square_y
+    zy, zyt = dot3(y, square_t), dot3(1.5 * y - 0.5 * square_y, square_t)
+    t_next = 1.5 * eye - 0.5 * zy
+    z, tail, square_t = dot3(t, t_next), dot3(zyt, t_next), dot3(t_next, t_next)
+    z = 1.5 * z - 0.5 * dot3(tail, square_t)
     return jnp.sqrt(d_col) * z * i_row / jnp.sqrt(fro)
 
 
@@ -84,11 +84,17 @@
 
 
 def owners(n_rows):
-    return (n_rows // 4, n_rows // 2) if n_rows % 4 == 0 else (0, n_rows)
+    if n_rows % 4:
+        return [(0, n_rows)] * 8
+    return [(n_rows // 4, n_rows // 2)] * 8
 
 
 def sizes_of(bw, n_own):
     return [2 * bw + 8 * n_own] * 2 + [bw] * 6
+
+
+def pieces_of(sizes, owned):
+    return [size // n_own for size, (_, n_own) in zip(sizes, owned)]
 
 
 def kernel(
@@ -109,9 +115,8 @@
     side = me // (n_rows // 2)
     partner = lax.rem(me + n_rows // 2, n_rows)
     partner_k = partner * n_pairs + group
-    first, n_own = owners(n_rows)
-    owner = (me >= first) & (me < first + n_own)
-    sizes = sizes_of(bw, n_own)
+    owned = owners(n_rows)
+    sizes = sizes_of(bw, owned[0][1])
 
     def fetches(half, c):
         cols = pl.ds(half * 2 * bw, 2 * bw)
@@ -167,7 +172,12 @@
         return total[:bw, :bw] + (total[:bw, bw:] + total[bw:, :bw])
 
     def place(b):
-        return sum(sizes[:b]), sum(sizes[:b]) // n_own, sizes[b] // n_own
+        pieces = pieces_of(sizes, owned)
+        return sum(sizes[:b]), sum(pieces[:b]), pieces[b]
+
+    def owner(b):
+        first, n_own = owned[b]
+        return (me >= first) & (me < first + n_own)
 
     def own(b, q):
         base, _, piece = place(b)
@@ -181,6 +191,7 @@
 
     def reduce_start(b, blocks=()):
         _, lbase, piece = place(b)
+        first, n_own = owned[b]
         fill_pay(b, blocks)
         if b == 0:
             pl.semaphore_wait(barrier, n - 1)
@@ -208,10 +219,10 @@
     def reduce_mid(b):
         _, lbase, piece = place(b)
 
-        @pl.when(owner)
+        @pl.when(owner(b))
         def _():
             wait_pieces(b, n_rows - 1, rs_r.at[b])
-            mine = own(b, me - first)
+            mine = own(b, me - owned[b][0])
             total = pay[mine, :]
             for off in range(1, n_rows):
                 total += land[off, lbase : lbase + piece, :]
@@ -228,13 +239,14 @@
             lax.fori_loop(1, n_rows, gather, 0)
 
     def pieces_to_owners(b, sem):
-        @pl.when(owner)
-        def _():
-            wait_pieces(b, n_own - 1, sem)
-
-        @pl.when(jnp.logical_not(owner))
-        def _():
-            wait_pieces(b, n_own, sem)
+        @pl.when(owner(b))
+        def _():
+            if owned[b][1] > 1:
+                wait_pieces(b, owned[b][1] - 1, sem)
+
+        @pl.when(jnp.logical_not(owner(b)))
+        def _():
+            wait_pieces(b, owned[b][1], sem)
 
     def reduce_end(b):
         base, _, _ = place(b)
@@ -244,7 +256,7 @@
     def settle(b):
         pieces_to_owners(b, rs_s.at[b])
 
-        @pl.when(owner)
+        @pl.when(owner(b))
         def _():
             wait_pieces(b, n_rows - 1, ag_s.at[b])
 
@@ -306,8 +318,6 @@
         vg = dot3(v, gram)
         return dot3(vg[:bw], v[:bw], NT), dot3(vg[bw:], v[bw:], NT)
 
-    n_early = early // 128
-
     def far_copy(half, j, at, size):
         return pltpu.make_async_remote_copy(
             x.at[3, 2 * half + j, :, pl.ds(at, size)], far.at[j, :, pl.ds(at, size)],
@@ -317,11 +327,15 @@
     shipped = [0, 0]
 
     def ship(half, some):
-        for i in range(shipped[half], min(shipped[half] + some, 2 * n_early)):
-            @pl.when(side != half)
-            def _():
+        n_early = early[half] // 128
+        upto = min(shipped[half] + some, 2 * n_early)
+
+        @pl.when(side != half)
+        def _():
+            for i in range(shipped[half], upto):
                 far_copy(half, i // n_early, i % n_early * 128, 128).start()
-        shipped[half] += some
+
+        shipped[half] = upto
 
     def scale_last(half, v, gram):
         vg = dot3(v, gram)
@@ -354,7 +368,8 @@
             k = half * count + lax.rem(my_k + i, count)
             if not same:
                 pltpu.make_async_remote_copy(
-                    send.at[k, :, early:], out_ref.at[my_k, :, early:], out_s.at[1], out_r.at[1], **to(k)
+                    send.at[k, :, early[half] :], out_ref.at[my_k, :, early[half] :],
+                    out_s.at[1], out_r.at[1], **to(k)
                 ).start()
                 return carry
 
@@ -372,21 +387,22 @@
 
         lax.fori_loop(0, count, go, 0)
 
-    def deliver_onward():
+    def deliver_onward(half):
         def go(i, carry):
             at = lax.rem(my_k + i, count)
-            k = side * count + at
-            spot = out_ref.at[partner_k, :, :early]
+            k = half * count + at
+            some = onward.at[at, :, : early[half]]
+            spot = out_ref.at[partner_k, :, : early[half]]
 
             @pl.when(k != my_k)
             def _():
                 pltpu.make_async_remote_copy(
-                    onward.at[at], spot, out_s.at[2], out_r.at[2], **to(k)
+                    some, spot, out_s.at[2], out_r.at[2], **to(k)
                 ).start()
 
             @pl.when(k == my_k)
             def _():
-                pltpu.make_async_copy(onward.at[at], spot, own_sem.at[1]).start()
+                pltpu.make_async_copy(some, spot, own_sem.at[1]).start()
 
             return carry
 
@@ -394,24 +410,25 @@
 
     def compute_last(half):
         s, m = x.at[3, 2 * half], x.at[3, 2 * half + 1]
-        finish(half, send, half * count, s, m, early, rows)
+        finish(half, send, half * count, s, m, early[half], rows)
 
         @pl.when(side == half)
         def _():
-            finish(half, send, half * count, s, m, 0, early)
-
-    def deliver_last(half):
+            finish(half, send, half * count, s, m, 0, early[half])
+
+    def deliver_other(half):
         @pl.when(side != half)
         def _():
             deliver(half, False)
 
+    def deliver_own(half):
         @pl.when(side == half)
         def _():
             deliver(half, True)
 
-    reduce_start(0, pack(fill_gram(1), n_own))
+    reduce_start(0, pack(fill_gram(1), owned[0][1]))
     raw_copy.start()
-    fill_pay(1, pack(fill_gram(0), n_own))
+    fill_pay(1, pack(fill_gram(0), owned[1][1]))
     reduce_start(1)
     reduce_mid(0)
     reduce_mid(1)
@@ -454,12 +471,12 @@
     put(split(va[:bw]), x.at[1, 0], x.at[1, 1], into(x.at[2, 0]))
     as_, am = new_grams(va, ga)
     reduce_mid(4)
+    gb = join(bs, reduce_end(4), am)
+    vb = whitening_t(gb)
+    put_and_pass(2, vb[bw:], x.at[2, 2], x.at[2, 3])
     for c in sent[1]:
         c.wait_recv()
     reduce_start(5, [cross_gram(x.at[2, 0], x.at[2, 1])])
-    gb = join(bs, reduce_end(4), am)
-    vb = whitening_t(gb)
-    put_and_pass(2, vb[bw:], x.at[2, 2], x.at[2, 3])
     bs, bm = new_grams(vb, gb)
     sent.append(pass_gram(2, bm))
     put(split(vb[:bw]), x.at[2, 2], x.at[2, 3], into(x.at[3, 2]))
@@ -477,7 +494,7 @@
     as_, am = new_grams(va, ga)
     reduce_mid(6)
     ship(1, SHIP[4])
-    ship(0, min(SHIP[5], n_early - SHIP[3]))
+    ship(0, min(SHIP[5], early[0] // 128 - SHIP[3]))
     for c in sent[2]:
         c.wait_recv()
     reduce_start(7, [cross_gram(x.at[3, 0], x.at[3, 1])])
@@ -487,20 +504,22 @@
     scale_last(1, whitening_t(gb), gb)
     compute_last(1)
     reduce_mid(7)
-    ship(1, 2 * n_early)
-    ship(0, 2 * n_early)
+    ship(1, 2 * early[1] // 128)
+    ship(0, 2 * early[0] // 128)
     ga = join(as_, reduce_end(7), gmm_in[2])
-    deliver_last(1)
+    deliver_other(1)
+    deliver_own(1)
     scale_last(0, whitening_t(ga), ga)
     compute_last(0)
-    deliver_last(0)
+    deliver_other(0)
+    deliver_own(0)
     for half in (1, 0):
         @pl.when(side == half)
         def _():
             for j in range(2):
-                far_copy(half, j, 0, early).wait_recv()
-            finish(half, onward, 0, far.at[0], far.at[1], 0, early)
-            deliver_onward()
+                far_copy(half, j, 0, early[half]).wait_recv()
+            finish(half, onward, 0, far.at[0], far.at[1], 0, early[half])
+            deliver_onward(half)
 
     for b in range(len(sizes)):
         settle(b)
@@ -510,17 +529,23 @@
     raw_copy.wait_send()
     v_pass.wait_send()
     v_share.wait_send()
-    for j in range(2):
-        far_copy(0, j, 0, early).wait_send()
     pltpu.make_async_copy(send.at[0], out_ref.at[my_k], own_sem.at[0]).wait()
-    pltpu.make_async_copy(onward.at[0], out_ref.at[my_k, :, :early], own_sem.at[1]).wait()
-    for ref, sems in ((send, out_s), (out_ref, out_r)):
-        for i, some in enumerate((
-            ref.at[pl.ds(0, count - 1)],
-            ref.at[pl.ds(0, count), :, early:],
-            ref.at[pl.ds(0, count - 1), :, :early],
-        )):
-            pltpu.make_async_copy(some, some, sems.at[i]).wait()
+
+    def done(ref, sem):
+        pltpu.make_async_copy(ref, ref, sem).wait()
+
+    for half in (0, 1):
+        @pl.when(side == half)
+        def _():
+            for j in range(2):
+                far_copy(1 - half, j, 0, early[1 - half]).wait_send()
+            done(onward.at[0, :, : early[half]], own_sem.at[1])
+            done(send.at[pl.ds(0, count - 1)], out_s.at[0])
+            done(send.at[pl.ds(0, count), :, early[1 - half] :], out_s.at[1])
+            done(onward.at[pl.ds(0, count - 1), :, : early[half]], out_s.at[2])
+            done(out_ref.at[pl.ds(0, count - 1)], out_r.at[0])
+            done(out_ref.at[pl.ds(0, count), :, early[half] :], out_r.at[1])
+            done(out_ref.at[pl.ds(0, count - 1), :, : early[half]], out_r.at[2])
 
 
 def interleave(in_ref, out_ref, taken, mixed, in_sem, out_sem):
@@ -540,7 +565,8 @@
         copy.wait()
 
 
-SHIP = (1, 1, 2, 1, 1, 3, 2, 1)
+EARLY = (4, 4)
+SHIP = (1, 1, 2, 1, 1, 2, 1, 1)
 
 
 def on_device(observed, estimate, mask, threshold):
@@ -551,10 +577,10 @@
     n = n_rows * n_pairs
     each = width // n
     step = 512 if rows % 512 == 0 else rows
-    early = rows * 4 // 12 // 128 * 128 or rows
+    early = [rows * part // 12 // 128 * 128 or rows for part in EARLY]
     ahead = rows * 5 // 12 // 128 * 128 or rows
-    n_own = owners(n_rows)[1]
-    sizes = sizes_of(bw, n_own)
+    owned = owners(n_rows)
+    sizes = sizes_of(bw, owned[0][1])
     total = sum(sizes)
     vmem = pl.BlockSpec(memory_space=pltpu.VMEM)
     dma = pltpu.SemaphoreType.DMA
@@ -571,15 +597,15 @@
             pltpu.VMEM((4, 4, bw, rows), F32),
             pltpu.VMEM((3, bw, rows), F32),
             pltpu.VMEM((total, bw), F32),
-            pltpu.VMEM((n_rows, total // n_own, bw), F32),
+            pltpu.VMEM((n_rows, sum(pieces_of(sizes, owned)), bw), F32),
             pltpu.VMEM((total, bw), F32),
             pltpu.VMEM((3, bw, bw), F32),
             pltpu.VMEM((3, bw, bw), F32),
             pltpu.VMEM((2, 2 * bw, 2 * bw), BF16),
             pltpu.VMEM((2, 2 * bw, 2 * bw), BF16),
             pltpu.VMEM((n, each, rows), F32),
-            pltpu.VMEM((2, bw, early), F32),
-            pltpu.VMEM((n // 2, each, early), F32),
+            pltpu.VMEM((2, bw, max(early)), F32),
+            pltpu.VMEM((n // 2, each, max(early)), F32),
             pltpu.VMEM((2, bw, ahead), F32),
             pltpu.VMEM((bw, 2 * bw), F32),
             pltpu.VMEM((bw, 2 * bw), F32),

time: 150 us -> 149 us (level)
  Pallas kernels: 150 us -> 148 us
    pallas_call x1, Pallas kernels: 147 us -> 146 us  [on_device(): pl.pallas_call(functools.partial(kernel, n_rows, n_pairs, step, early, ah...]
where the time goes in v3:
time: 149 us
  Pallas kernels  148 us (99%)
    pallas_call x1, Pallas kernels, on_device(): pl.pallas_call(functools.partial(kernel, n_rows, n_pairs, step, early, ah...  146 us

profile of v3, /device:TPU:0, one launch (start us, length us, event | category | flops | bytes accessed | tf_op | source)
XLA Modules:
  0.0 148.6 jit_solution(16814555078721037525)
XLA Ops:
  0.0 145.5 %shard_map.46 = f32[32,16,1536]{2,1,0:T(8,128)} custom-call(f32[1536,512]{1,0:T(8,128)} %obs_ref.1, f32[1536,512]{1,0:T(8,128)} %est_ref.1, s32[1536,512]{1,0:T(8,128)} %mask_ref.1, f32[1,512]{1,0:T(1,128)} %bitcast.3), custom_call_target="tpu_custom_call" | custom-call | tf_op jit(solution)/shard_map/pallas_call | solution.py:588
  145.5 2.9 %shard_map.47 = f32[64,12288]{1,0:T(8,128)} custom-call(f32[8,4,16,1536]{3,2,1,0:T(8,128)} %bitcast.2), custom_call_target="tpu_custom_call" | custom-call | tf_op jit(solution)/shard_map/pallas_call | solution.py:622

commit v4 on v3

--- a/solution.py
+++ b/solution.py
@@ -351,8 +351,8 @@
 
     per_block = bw // each
 
-    def finish(half, target, base, s, m, start, stop):
-        for j in range(2):
+    def finish(half, target, base, s, m, start, stop, slots=(0, 1)):
+        for j in slots:
             def write(part, value):
                 for i in range(per_block):
                     target[base + j * per_block + i, :, part] = value[i * each : (i + 1) * each]
@@ -363,9 +363,9 @@
     def to(k):
         return dict(device_id=(k // n_pairs, lax.rem(k, n_pairs)), device_id_type=MESH)
 
-    def deliver(half, same):
+    def deliver(half, same, begin=0, some=count):
         def go(i, carry):
-            k = half * count + lax.rem(my_k + i, count)
+            k = half * count + begin + lax.rem(my_k + i, some)
             if not same:
                 pltpu.make_async_remote_copy(
                     send.at[k, :, early[half] :], out_ref.at[my_k, :, early[half] :],
@@ -385,7 +385,7 @@
 
             return carry
 
-        lax.fori_loop(0, count, go, 0)
+        lax.fori_loop(0, some, go, 0)
 
     def deliver_onward(half):
         def go(i, carry):
@@ -510,9 +510,18 @@
     deliver_other(1)
     deliver_own(1)
     scale_last(0, whitening_t(ga), ga)
-    compute_last(0)
-    deliver_other(0)
-    deliver_own(0)
+    for j in range(2):
+        finish(0, send, 0, x.at[3, 0], x.at[3, 1], early[0], rows, (j,))
+
+        @pl.when(side != 0)
+        def _():
+            deliver(0, False, j * per_block, per_block)
+
+        @pl.when(side == 0)
+        def _():
+            finish(0, send, 0, x.at[3, 0], x.at[3, 1], 0, early[0], (j,))
+            deliver(0, True, j * per_block, per_block)
+
     for half in (1, 0):
         @pl.when(side == half)
         def _():

time: 149 us -> 149 us (level)
  no operation moved by 1% of the time
where the time goes in v4:
time: 149 us; the launch traced here: 147 us
  Pallas kernels  147 us (99%)
    pallas_call x1, Pallas kernels, on_device(): pl.pallas_call(functools.partial(kernel, n_rows, n_pairs, step, early, ah...  144 us

profile of v4, /device:TPU:0, one launch (start us, length us, event | category | flops | bytes accessed | tf_op | source)
XLA Modules:
  0.0 147.5 jit_solution(2953309649460234797)
XLA Ops:
  0.0 144.4 %shard_map.46 = f32[32,16,1536]{2,1,0:T(8,128)} custom-call(f32[1536,512]{1,0:T(8,128)} %obs_ref.1, f32[1536,512]{1,0:T(8,128)} %est_ref.1, s32[1536,512]{1,0:T(8,128)} %mask_ref.1, f32[1,512]{1,0:T(1,128)} %bitcast.3), custom_call_target="tpu_custom_call" | custom-call | tf_op jit(solution)/shard_map/pallas_call | solution.py:597
  144.4 2.9 %shard_map.47 = f32[64,12288]{1,0:T(8,128)} custom-call(f32[8,4,16,1536]{3,2,1,0:T(8,128)} %bitcast.2), custom_call_target="tpu_custom_call" | custom-call | tf_op jit(solution)/shard_map/pallas_call | solution.py:631
